TPU v7x, 32 devices: a whole 2x2x4 slice. The times are simulated.
32 devices in a mesh: fits: 2 (over y), tm: 4 (over z), space: 4 (over x, core).
Axes of the slice: x: 2, y: 2, z: 4, core: 2. Of those that a mesh axis runs over, the one named last changes fastest.
Arguments:
- coupling: float32 [16, 4, 384, 384], P(('fits', 'tm'), 'space'), parts along dimension 0, may hold values from -0.034701105 to 1.0347011, as said below
- schur_inverse: float32 [16, 4, 384, 384], P(('fits', 'tm'), 'space'), parts along dimension 0, may hold values from -0.052051657 to 1.0720517, as said below
- entry_rows: int32 [16, 4, 2048], P(('fits', 'tm'), 'space'), parts along dimension 0, may hold values from 0 to 383
- entry_shift: int32 [16, 4, 2048], P(('fits', 'tm'), 'space'), parts along dimension 0, may hold values from -3 to 3
- entry_hyper: int32 [16, 4, 2048], P(('fits', 'tm'), 'space'), parts along dimension 0, may hold values from 0 to 3
- entry_values: float32 [16, 4, 2048], P(('fits', 'tm'), 'space'), parts along dimension 0, may hold values from -0.3125 to 0.3125
Outputs:
- marginal_cov: float32 [16, 4, 384, 384], P(('fits', 'tm'), 'space'), parts along dimension 0
- gradient: float32 [8], P('fits'), parts along dimension 0
There are 2 independent parts, one for each index of `fits`. A program takes and returns all parts, laid end to end along the dimension named above; each array names one. Nothing has to cross between parts.
Inputs may be any that keep to these rules, and one draw needn't show every extreme that they name: Every block of coupling has entries within the stated range. Every block of schur_inverse is symmetric positive definite.
All inputs are finite; a program needn't handle non-finite values.
Results may differ from a plain program's by a relative error of at most 0.0001.
Values sent between devices are 32-bit elements; how exact they have to be, the bound alone decides.
A program may use at most 128 MiB of HBM per device.

v0:
```python
import jax
import jax.numpy as jnp
from jax import lax
from jax.sharding import PartitionSpec as P

NHYP = 4


def prefix(shard, axis, combine, identity):
    devices, mine = (lax.axis_size(axis), lax.axis_index(axis))
    everything = jax.tree.map(lambda part: lax.all_gather(part, axis), shard)
    start = jax.tree.map(
        lambda part, zero: jnp.broadcast_to(jnp.asarray(zero, part.dtype), part.shape),
        shard,
        identity,
    )

    def step(k, before):
        at = devices - 1 - k
        reached = at > mine
        new = combine(before, jax.tree.map(lambda part: part[at], everything))
        return jax.tree.map(lambda a, b: jnp.where(reached, a, b), new, before)

    return lax.fori_loop(0, devices, step, start)


def apply_map(coupling, schur_inverse, current):
    product = jnp.einsum("sij,sjk->sik", coupling, current, precision=lax.Precision.HIGHEST)
    return (
        jnp.einsum("sik,slk->sil", product, coupling, precision=lax.Precision.HIGHEST)
        + schur_inverse
    )


def combine_maps(earlier, later):
    joined_g = jnp.einsum("sij,sjk->sik", later[0], earlier[0], precision=lax.Precision.HIGHEST)
    joined_s = apply_map(later[0], later[1], earlier[1])
    return (joined_g, joined_s)


def on_device(coupling, schur_inverse, entry_rows, entry_shift, entry_hyper, entry_values):
    time_count = coupling.shape[0]
    order = coupling.shape[2]
    composite_g = coupling[time_count - 1]
    composite_s = schur_inverse[time_count - 1]
    position = 0
    composite_s = apply_map(coupling[position], schur_inverse[position], composite_s)
    composite_g = jnp.einsum(
        "sij,sjk->sik", coupling[position], composite_g, precision=lax.Precision.HIGHEST
    )
    identity = (
        jnp.broadcast_to(jnp.eye(order, dtype=jnp.float32), composite_g.shape),
        jnp.zeros_like(composite_s),
    )
    scanned = prefix((composite_g, composite_s), "tm", combine_maps, identity)
    boundary = scanned[1]
    results = [None] * time_count
    current = boundary
    for position in range(time_count - 1, -1, -1):
        current = apply_map(coupling[position], schur_inverse[position], current)
        results[position] = current
    marginal_cov = jnp.stack(results, axis=0)
    columns = jnp.mod(entry_rows + entry_shift, order)
    flat_index = entry_rows * order + columns
    flattened = marginal_cov.reshape(time_count, coupling.shape[1], order * order)
    picked = jnp.take_along_axis(flattened, flat_index, axis=2)
    one_hot = (entry_hyper[..., None] == jnp.arange(NHYP, dtype=jnp.int32)).astype(jnp.float32)
    local_terms = -0.5 * jnp.sum((entry_values * picked)[..., None] * one_hot, axis=(0, 1, 2))
    gradient = lax.psum(local_terms, ("tm", "space"))
    return (marginal_cov, gradient)


def solution(mesh):
    in_specs = (
        P(("fits", "tm"), "space", None, None),
        P(("fits", "tm"), "space", None, None),
        P(("fits", "tm"), "space", None),
        P(("fits", "tm"), "space", None),
        P(("fits", "tm"), "space", None),
        P(("fits", "tm"), "space", None),
    )
    out_specs = (P(("fits", "tm"), "space", None, None), P("fits"))
    return jax.shard_map(
        on_device, mesh=mesh, in_specs=in_specs, out_specs=out_specs, check_vma=False
    )
```

profile of v0, /device:TPU:0, one launch (start us, length us, event | category | flops | bytes accessed | tf_op | source)
XLA Modules:
  0.0 225.0 jit_solution(2873054929532404826)
XLA Ops:
  7.2 0.0 all-gather.7.cloned.1.call-start
  7.2 2.6 %fusion.16 = f32[384,384]{1,0:T(8,128)S(1)} fusion(f32[2,1,384,384]{3,2,1,0:T(8,128)} %param.9, f32[2,1,384,384]{3,2,1,0:T(8,128)} %param.8), kind=kOutput, calls=%fused_computation.23 | convolution fusion | flops 679477248 | bytes 1769472 | tf_op jit(solution)/shard_map/sij,sjk->sik/dot_general | solution.py:28
  9.8 3.1 %convolution_add_fusion.3 = f32[384,384]{1,0:T(8,128)} fusion(f32[384,384]{1,0:T(8,128)S(1)} %fusion.16, f32[2,1,384,384]{3,2,1,0:T(8,128)} %param.9, f32[2,1,384,384]{3,2,1,0:T(8,128)S(1)} %copy-done), kind=kOutput, calls=%fused_computation.18 | convolution fusion | flops 679624704 | bytes 2359296 | tf_op jit(solution)/shard_map/sik,slk->sil/dot_general | solution.py:30
  13.0 0.0 all-gather.7.cloned.1.call-update
  13.0 0.0 all-gather.5.cloned.1.call-start
  13.1 2.1 fusion.20
  15.2 0.0 all-gather.5.cloned.1.call-update
  15.2 0.6 copy.23
  15.8 0.7 bitcast_or_fusion
  16.5 49.3 %all-gather.7.cloned.1.call-done = f32[1536,384]{1,0:T(8,128)} async-done(((f32[384,384]{1,0:T(8,128)}), f32[1536,384]{1,0:T(8,128)}) %all-gather.7.cloned.1.call-update) | async-done | bytes 2359312 | tf_op jit(solution)/shard_map/all_gather | solution.py:11
  65.9 50.9 %all-gather.5.cloned.1.call-done = f32[1536,384]{1,0:T(8,128)} async-done(((f32[384,384]{1,0:T(8,128)}), f32[1536,384]{1,0:T(8,128)}) %all-gather.5.cloned.1.call-update) | async-done | bytes 2359312 | tf_op jit(solution)/shard_map/all_gather | solution.py:11
  116.8 19.9 %while.16 = (s32[]{:T(128)}, f32[1,384,384]{2,1,0:T(8,128)S(1)}, s32[]{:T(128)}, f32[4,1,384,384]{3,2,1,0:T(8,128)}, f32[4,1,384,384]{3,2,1,0:T(8,128)}, /*index=5*/s32[]{:T(128)}, s32[]{:T(128)}, s32[]{:T(128)}, s32[]{:T(128)}) while((s32[]{:T(128)}, f32[1,384,384]{2,1,0:T(8,128)S(1)}, s32[]{:T(128)}, ...), condition=%wide.region_1.2_spmd.clone, body=%wide.region_0.1_spmd.clone.sunk | while | flops 1359544320 | bytes 4720802 | solution.py:24
  116.8 2.3 %fusion.54 = f32[384,384]{1,0:T(8,128)S(1)} fusion(f32[1,384,384]{2,1,0:T(8,128)S(1)} %get-tuple-element.221, f32[4,1,384,384]{3,2,1,0:T(8,128)} %get-tuple-element.232, s32[]{:T(128)S(6)} %select_n.74, pred[]{:T(512)S(6)} %compare.3), kind=kOutput, calls=%fused_computation.4.clone.1 | convolution fusion | flops 679624704 | bytes 1769477 | tf_op jit(solution)/shard_map/while/body/eval_jaxpr/sij,sjk->sik/dot_general | solution.py:28
  119.1 2.6 %fusion.55 = f32[1,384,384]{2,1,0:T(8,128)S(1)} fusion(f32[384,384]{1,0:T(8,128)S(1)} %fusion.54, f32[4,1,384,384]{3,2,1,0:T(8,128)} %get-tuple-element.233, s32[]{:T(128)S(6)} %select_n.74, f32[1,384,384]{2,1,0:T(8,128)S(1)} %get-tuple-element.221, f32[4,1,384,384]{3,2,1,0:T(8,128)} %get-tuple-element.232, pred[]{:T(512)S(6)} %compare.3, pred[]{:T(512)S(6)} %gt.12), kind=kOutput, calls=%fused_computation.3.clone.1 | convolution fusion | flops 679919616 | bytes 2951168 | tf_op jit(solution)/shard_map/while/body/eval_jaxpr/sik,slk->sil/dot_general | solution.py:30
  121.8 2.3 %fusion.54 = f32[384,384]{1,0:T(8,128)S(1)} fusion(f32[1,384,384]{2,1,0:T(8,128)S(1)} %get-tuple-element.221, f32[4,1,384,384]{3,2,1,0:T(8,128)} %get-tuple-element.232, s32[]{:T(128)S(6)} %select_n.74, pred[]{:T(512)S(6)} %compare.3), kind=kOutput, calls=%fused_computation.4.clone.1 | convolution fusion | flops 679624704 | bytes 1769477 | tf_op jit(solution)/shard_map/while/body/eval_jaxpr/sij,sjk->sik/dot_general | solution.py:28
  124.1 2.6 %fusion.55 = f32[1,384,384]{2,1,0:T(8,128)S(1)} fusion(f32[384,384]{1,0:T(8,128)S(1)} %fusion.54, f32[4,1,384,384]{3,2,1,0:T(8,128)} %get-tuple-element.233, s32[]{:T(128)S(6)} %select_n.74, f32[1,384,384]{2,1,0:T(8,128)S(1)} %get-tuple-element.221, f32[4,1,384,384]{3,2,1,0:T(8,128)} %get-tuple-element.232, pred[]{:T(512)S(6)} %compare.3, pred[]{:T(512)S(6)} %gt.12), kind=kOutput, calls=%fused_computation.3.clone.1 | convolution fusion | flops 679919616 | bytes 2951168 | tf_op jit(solution)/shard_map/while/body/eval_jaxpr/sik,slk->sil/dot_general | solution.py:30
  126.7 2.3 %fusion.54 = f32[384,384]{1,0:T(8,128)S(1)} fusion(f32[1,384,384]{2,1,0:T(8,128)S(1)} %get-tuple-element.221, f32[4,1,384,384]{3,2,1,0:T(8,128)} %get-tuple-element.232, s32[]{:T(128)S(6)} %select_n.74, pred[]{:T(512)S(6)} %compare.3), kind=kOutput, calls=%fused_computation.4.clone.1 | convolution fusion | flops 679624704 | bytes 1769477 | tf_op jit(solution)/shard_map/while/body/eval_jaxpr/sij,sjk->sik/dot_general | solution.py:28
  129.1 2.6 %fusion.55 = f32[1,384,384]{2,1,0:T(8,128)S(1)} fusion(f32[384,384]{1,0:T(8,128)S(1)} %fusion.54, f32[4,1,384,384]{3,2,1,0:T(8,128)} %get-tuple-element.233, s32[]{:T(128)S(6)} %select_n.74, f32[1,384,384]{2,1,0:T(8,128)S(1)} %get-tuple-element.221, f32[4,1,384,384]{3,2,1,0:T(8,128)} %get-tuple-element.232, pred[]{:T(512)S(6)} %compare.3, pred[]{:T(512)S(6)} %gt.12), kind=kOutput, calls=%fused_computation.3.clone.1 | convolution fusion | flops 679919616 | bytes 2951168 | tf_op jit(solution)/shard_map/while/body/eval_jaxpr/sik,slk->sil/dot_general | solution.py:30
  131.7 2.3 %fusion.54 = f32[384,384]{1,0:T(8,128)S(1)} fusion(f32[1,384,384]{2,1,0:T(8,128)S(1)} %get-tuple-element.221, f32[4,1,384,384]{3,2,1,0:T(8,128)} %get-tuple-element.232, s32[]{:T(128)S(6)} %select_n.74, pred[]{:T(512)S(6)} %compare.3), kind=kOutput, calls=%fused_computation.4.clone.1 | convolution fusion | flops 679624704 | bytes 1769477 | tf_op jit(solution)/shard_map/while/body/eval_jaxpr/sij,sjk->sik/dot_general | solution.py:28
  134.1 2.6 %fusion.55 = f32[1,384,384]{2,1,0:T(8,128)S(1)} fusion(f32[384,384]{1,0:T(8,128)S(1)} %fusion.54, f32[4,1,384,384]{3,2,1,0:T(8,128)} %get-tuple-element.233, s32[]{:T(128)S(6)} %select_n.74, f32[1,384,384]{2,1,0:T(8,128)S(1)} %get-tuple-element.221, f32[4,1,384,384]{3,2,1,0:T(8,128)} %get-tuple-element.232, pred[]{:T(512)S(6)} %compare.3, pred[]{:T(512)S(6)} %gt.12), kind=kOutput, calls=%fused_computation.3.clone.1 | convolution fusion | flops 679919616 | bytes 2951168 | tf_op jit(solution)/shard_map/while/body/eval_jaxpr/sik,slk->sil/dot_general | solution.py:30
  136.7 2.0 fusion.14
  138.8 2.0 convolution_add_fusion.2
  140.8 2.9 %fusion.23 = f32[384,384]{1,0:T(8,128)} fusion(f32[384,384]{1,0:T(8,128)S(1)} %convolution_add_fusion.2, f32[2,1,384,384]{3,2,1,0:T(8,128)S(1)} %copy-done), kind=kOutput, calls=%fused_computation.30 | convolution fusion | flops 679477248 | bytes 1769472 | tf_op jit(solution)/shard_map/sij,sjk->sik/dot_general | solution.py:28
  143.7 1.4 stack.19
  145.1 3.1 %convolution_add_fusion.1 = f32[384,384]{1,0:T(8,128)S(1)} fusion(f32[384,384]{1,0:T(8,128)} %fusion.23, f32[2,1,384,384]{3,2,1,0:T(8,128)S(1)} %copy-done.1, f32[2,1,384,384]{3,2,1,0:T(8,128)S(1)} %copy-done), kind=kOutput, calls=%fused_computation.16 | convolution fusion | flops 679624704 | bytes 2359296 | tf_op jit(solution)/shard_map/sik,slk->sil/dot_general | solution.py:30
  148.2 0.6 stack.18
  148.8 0.5 copy-done.2
  149.2 1.1 maximum_bitcast_fusion
  150.4 34.9 %gather_fusion = f32[4096]{0:T(1024)S(1)} fusion(f32[2,147456]{1,0:T(2,128)S(1)} %maximum_bitcast_fusion, s32[4096]{0:T(1024)S(1)} %bitcast.81), kind=kCustom, calls=%fused_computation | custom fusion | bytes 65536 | tf_op jit(solution)/shard_map/jit(take_along_axis)/gather | solution.py:66
  185.4 0.1 select_reduce_fusion
  185.5 31.6 %psum.7 = f32[4]{0:T(128)} all-reduce(f32[4]{0:T(128)S(1)} %broadcast_multiply_fusion), channel_id=1, replica_groups=mesh['fits'=2,'tm'=4,'space'=4] {'tm','space'}, use_global_device_ids=true, to_apply=%region_3.4 | all-reduce | flops 4 | bytes 32 | tf_op jit(solution)/shard_map/psum | solution.py:69
  217.1 1.1 pad_maximum_fusion
  (21 shorter events, 0.1 us)
Async XLA Ops:
  7.2 2.7 %copy-start = (f32[2,1,384,384]{3,2,1,0:T(8,128)S(1)}, f32[2,1,384,384]{3,2,1,0:T(8,128)}, u32[]{:S(2)}) copy-start(f32[2,1,384,384]{3,2,1,0:T(8,128)} %param.8) | copy-start | bytes 3538948
  7.2 58.7 %all-gather.7.cloned.1.call-start = ((), (), s32[]{:S(2)}) async-start(), calls=%async_computation.1 | async-start | bytes 2949120 | tf_op jit(solution)/shard_map/all_gather | solution.py:11
  13.0 2.2 copy-start.5
  13.0 2.8 %copy-start.6 = (s32[2,1,2048]{2,1,0:T(1,128)S(1)}, s32[2,1,2048]{2,1,0:T(1,128)}, u32[]{:S(2)}) copy-start(s32[2,1,2048]{2,1,0:T(1,128)} %param.10) | copy-start | bytes 49156
  13.0 2.8 %copy-start.7 = (s32[2,1,2048]{2,1,0:T(1,128)S(1)}, s32[2,1,2048]{2,1,0:T(1,128)}, u32[]{:S(2)}) copy-start(s32[2,1,2048]{2,1,0:T(1,128)} %param.11) | copy-start | bytes 49156
  13.0 103.7 %all-gather.5.cloned.1.call-start = ((), (), s32[]{:S(2)}) async-start(), calls=%async_computation | async-start | bytes 2949120 | tf_op jit(solution)/shard_map/all_gather | solution.py:11
  136.7 2.1 copy-start.1
  148.2 1.1 copy-start.2
  150.4 35.0 %copy-start.4 = (s32[2,1,2048]{2,1,0:T(1,128)S(1)}, s32[2,1,2048]{2,1,0:T(1,128)}, u32[]{:S(2)}) copy-start(s32[2,1,2048]{2,1,0:T(1,128)} %get-tuple-element.179) | copy-start | bytes 49156
  150.4 35.0 %copy-start.8 = (f32[2,1,2048]{2,1,0:T(1,128)S(1)}, f32[2,1,2048]{2,1,0:T(1,128)}, u32[]{:S(2)}) copy-start(f32[2,1,2048]{2,1,0:T(1,128)} %param.13) | copy-start | bytes 49156
  150.4 35.0 %copy-start.3 = (s32[2,1,2048]{2,0,1:T(2,128)S(1)}, s32[2,1,2048]{2,0,1:T(2,128)}, u32[]{:S(2)}) copy-start(s32[2,1,2048]{2,0,1:T(2,128)} %copy.23) | copy-start | bytes 49156
Sparse Core Ops, SparseCore 0:
  13.1 52.6 all-gather.6
  68.0 48.7 all-gather.4
where the time goes:
time: 226 us; the launch traced here: 225 us
  waiting for transfers between devices  100 us (44%)
  local copies, waits for them, and re-layouts  38 us (17%)
  matrix products  37.6 us (17%)
  blocking collectives  31.6 us (14%)
  between operations  14.3 us (6%)
  other arithmetic  3.1 us (1%)
    all_gather x2, waiting for transfers between devices, prefix(): everything = jax.tree.map(lambda part: lax.all_gather(part, axis), shard)  100 us
    gather x1, local copies, waits for them, and re-layouts, on_device(): picked = jnp.take_along_axis(flattened, flat_index, axis=2)  34.9 us
    psum x1, blocking collectives, on_device(): gradient = lax.psum(local_terms, ('tm', 'space'))  31.6 us
    dot_general x7, matrix products, apply_map(): jnp.einsum('sik,slk->sil', product, coupling, precision=lax.Precision.HIG...  18.8 us
    dot_general x7, matrix products, apply_map(): jnp.einsum('sij,sjk->sik', coupling, current, precision=lax.Precision.HIG...  16.8 us
  transfers between devices with their start and end apart: 2, of which 2 were waited for; matrix products, arithmetic and copies ran while one was open for 2% of the time, Pallas kernels for 0%

commit v1 on v0

--- a/solution.py
+++ b/solution.py
@@ -66,7 +66,7 @@
     picked = jnp.take_along_axis(flattened, flat_index, axis=2)
     one_hot = (entry_hyper[..., None] == jnp.arange(NHYP, dtype=jnp.int32)).astype(jnp.float32)
     local_terms = -0.5 * jnp.sum((entry_values * picked)[..., None] * one_hot, axis=(0, 1, 2))
-    gradient = lax.psum(local_terms, ("tm", "space"))
+    gradient = lax.psum(lax.psum(local_terms, "space"), "tm")
     return (marginal_cov, gradient)
 
 

time: 226 us -> 211 us (0.934)
  blocking collectives: 31.6 us -> 16.8 us
    psum x1 -> x2, blocking collectives: 31.6 us -> 16.8 us  [on_device(): gradient = lax.psum(lax.psum(local_terms, 'space'), 'tm')]
where the time goes in v1:
time: 211 us; the launch traced here: 210 us
  waiting for transfers between devices  100 us (47%)
  local copies, waits for them, and re-layouts  38 us (18%)
  matrix products  37.6 us (18%)
  blocking collectives  16.8 us (8%)
  between operations  14.3 us (7%)
  other arithmetic  3.09 us (1%)
    all_gather x2, waiting for transfers between devices, prefix(): everything = jax.tree.map(lambda part: lax.all_gather(part, axis), shard)  100 us
    gather x1, local copies, waits for them, and re-layouts, on_device(): picked = jnp.take_along_axis(flattened, flat_index, axis=2)  34.9 us
    dot_general x7, matrix products, apply_map(): jnp.einsum('sik,slk->sil', product, coupling, precision=lax.Precision.HIG...  18.8 us
    psum x2, blocking collectives, on_device(): gradient = lax.psum(lax.psum(local_terms, 'space'), 'tm')  16.8 us
    dot_general x7, matrix products, apply_map(): jnp.einsum('sij,sjk->sik', coupling, current, precision=lax.Precision.HIG...  16.8 us
  transfers between devices with their start and end apart: 2, of which 2 were waited for; matrix products, arithmetic and copies ran while one was open for 2% of the time, Pallas kernels for 0%

profile of v1, /device:TPU:0, one launch (start us, length us, event | category | flops | bytes accessed | tf_op | source)
XLA Modules:
  0.0 210.3 jit_solution(7050171508525071041)
XLA Ops:
  7.2 0.0 all-gather.7.cloned.1.call-start
  7.2 2.6 %fusion.16 = f32[384,384]{1,0:T(8,128)S(1)} fusion(f32[2,1,384,384]{3,2,1,0:T(8,128)} %param.9, f32[2,1,384,384]{3,2,1,0:T(8,128)} %param.8), kind=kOutput, calls=%fused_computation.23 | convolution fusion | flops 679477248 | bytes 1769472 | tf_op jit(solution)/shard_map/sij,sjk->sik/dot_general | solution.py:28
  9.8 3.2 %convolution_add_fusion.3 = f32[384,384]{1,0:T(8,128)} fusion(f32[384,384]{1,0:T(8,128)S(1)} %fusion.16, f32[2,1,384,384]{3,2,1,0:T(8,128)} %param.9, f32[2,1,384,384]{3,2,1,0:T(8,128)S(1)} %copy-done), kind=kOutput, calls=%fused_computation.18 | convolution fusion | flops 679624704 | bytes 2359296 | tf_op jit(solution)/shard_map/sik,slk->sil/dot_general | solution.py:30
  13.0 0.0 all-gather.7.cloned.1.call-update
  13.0 0.0 all-gather.5.cloned.1.call-start
  13.1 2.1 fusion.20
  15.2 0.6 copy.23
  15.8 0.7 bitcast_or_fusion
  16.5 49.3 %all-gather.7.cloned.1.call-done = f32[1536,384]{1,0:T(8,128)} async-done(((f32[384,384]{1,0:T(8,128)}), f32[1536,384]{1,0:T(8,128)}) %all-gather.7.cloned.1.call-update) | async-done | bytes 2359312 | tf_op jit(solution)/shard_map/all_gather | solution.py:11
  65.9 50.9 %all-gather.5.cloned.1.call-done = f32[1536,384]{1,0:T(8,128)} async-done(((f32[384,384]{1,0:T(8,128)}), f32[1536,384]{1,0:T(8,128)}) %all-gather.5.cloned.1.call-update) | async-done | bytes 2359312 | tf_op jit(solution)/shard_map/all_gather | solution.py:11
  116.8 19.9 %while.16 = (s32[]{:T(128)}, f32[1,384,384]{2,1,0:T(8,128)S(1)}, s32[]{:T(128)}, f32[4,1,384,384]{3,2,1,0:T(8,128)}, f32[4,1,384,384]{3,2,1,0:T(8,128)}, /*index=5*/s32[]{:T(128)}, s32[]{:T(128)}, s32[]{:T(128)}, s32[]{:T(128)}) while((s32[]{:T(128)}, f32[1,384,384]{2,1,0:T(8,128)S(1)}, s32[]{:T(128)}, ...), condition=%wide.region_1.2_spmd.clone, body=%wide.region_0.1_spmd.clone.sunk | while | flops 1359544320 | bytes 4720802 | solution.py:24
  116.8 2.3 %fusion.54 = f32[384,384]{1,0:T(8,128)S(1)} fusion(f32[1,384,384]{2,1,0:T(8,128)S(1)} %get-tuple-element.221, f32[4,1,384,384]{3,2,1,0:T(8,128)} %get-tuple-element.232, s32[]{:T(128)S(6)} %select_n.74, pred[]{:T(512)S(6)} %compare.3), kind=kOutput, calls=%fused_computation.4.clone.1 | convolution fusion | flops 679624704 | bytes 1769477 | tf_op jit(solution)/shard_map/while/body/eval_jaxpr/sij,sjk->sik/dot_general | solution.py:28
  119.1 2.6 %fusion.55 = f32[1,384,384]{2,1,0:T(8,128)S(1)} fusion(f32[384,384]{1,0:T(8,128)S(1)} %fusion.54, f32[4,1,384,384]{3,2,1,0:T(8,128)} %get-tuple-element.233, s32[]{:T(128)S(6)} %select_n.74, f32[1,384,384]{2,1,0:T(8,128)S(1)} %get-tuple-element.221, f32[4,1,384,384]{3,2,1,0:T(8,128)} %get-tuple-element.232, pred[]{:T(512)S(6)} %compare.3, pred[]{:T(512)S(6)} %gt.12), kind=kOutput, calls=%fused_computation.3.clone.1 | convolution fusion | flops 679919616 | bytes 2951168 | tf_op jit(solution)/shard_map/while/body/eval_jaxpr/sik,slk->sil/dot_general | solution.py:30
  121.8 2.3 %fusion.54 = f32[384,384]{1,0:T(8,128)S(1)} fusion(f32[1,384,384]{2,1,0:T(8,128)S(1)} %get-tuple-element.221, f32[4,1,384,384]{3,2,1,0:T(8,128)} %get-tuple-element.232, s32[]{:T(128)S(6)} %select_n.74, pred[]{:T(512)S(6)} %compare.3), kind=kOutput, calls=%fused_computation.4.clone.1 | convolution fusion | flops 679624704 | bytes 1769477 | tf_op jit(solution)/shard_map/while/body/eval_jaxpr/sij,sjk->sik/dot_general | solution.py:28
  124.1 2.6 %fusion.55 = f32[1,384,384]{2,1,0:T(8,128)S(1)} fusion(f32[384,384]{1,0:T(8,128)S(1)} %fusion.54, f32[4,1,384,384]{3,2,1,0:T(8,128)} %get-tuple-element.233, s32[]{:T(128)S(6)} %select_n.74, f32[1,384,384]{2,1,0:T(8,128)S(1)} %get-tuple-element.221, f32[4,1,384,384]{3,2,1,0:T(8,128)} %get-tuple-element.232, pred[]{:T(512)S(6)} %compare.3, pred[]{:T(512)S(6)} %gt.12), kind=kOutput, calls=%fused_computation.3.clone.1 | convolution fusion | flops 679919616 | bytes 2951168 | tf_op jit(solution)/shard_map/while/body/eval_jaxpr/sik,slk->sil/dot_general | solution.py:30
  126.8 2.3 %fusion.54 = f32[384,384]{1,0:T(8,128)S(1)} fusion(f32[1,384,384]{2,1,0:T(8,128)S(1)} %get-tuple-element.221, f32[4,1,384,384]{3,2,1,0:T(8,128)} %get-tuple-element.232, s32[]{:T(128)S(6)} %select_n.74, pred[]{:T(512)S(6)} %compare.3), kind=kOutput, calls=%fused_computation.4.clone.1 | convolution fusion | flops 679624704 | bytes 1769477 | tf_op jit(solution)/shard_map/while/body/eval_jaxpr/sij,sjk->sik/dot_general | solution.py:28
  129.1 2.6 %fusion.55 = f32[1,384,384]{2,1,0:T(8,128)S(1)} fusion(f32[384,384]{1,0:T(8,128)S(1)} %fusion.54, f32[4,1,384,384]{3,2,1,0:T(8,128)} %get-tuple-element.233, s32[]{:T(128)S(6)} %select_n.74, f32[1,384,384]{2,1,0:T(8,128)S(1)} %get-tuple-element.221, f32[4,1,384,384]{3,2,1,0:T(8,128)} %get-tuple-element.232, pred[]{:T(512)S(6)} %compare.3, pred[]{:T(512)S(6)} %gt.12), kind=kOutput, calls=%fused_computation.3.clone.1 | convolution fusion | flops 679919616 | bytes 2951168 | tf_op jit(solution)/shard_map/while/body/eval_jaxpr/sik,slk->sil/dot_general | solution.py:30
  131.7 2.3 %fusion.54 = f32[384,384]{1,0:T(8,128)S(1)} fusion(f32[1,384,384]{2,1,0:T(8,128)S(1)} %get-tuple-element.221, f32[4,1,384,384]{3,2,1,0:T(8,128)} %get-tuple-element.232, s32[]{:T(128)S(6)} %select_n.74, pred[]{:T(512)S(6)} %compare.3), kind=kOutput, calls=%fused_computation.4.clone.1 | convolution fusion | flops 679624704 | bytes 1769477 | tf_op jit(solution)/shard_map/while/body/eval_jaxpr/sij,sjk->sik/dot_general | solution.py:28
  134.1 2.6 %fusion.55 = f32[1,384,384]{2,1,0:T(8,128)S(1)} fusion(f32[384,384]{1,0:T(8,128)S(1)} %fusion.54, f32[4,1,384,384]{3,2,1,0:T(8,128)} %get-tuple-element.233, s32[]{:T(128)S(6)} %select_n.74, f32[1,384,384]{2,1,0:T(8,128)S(1)} %get-tuple-element.221, f32[4,1,384,384]{3,2,1,0:T(8,128)} %get-tuple-element.232, pred[]{:T(512)S(6)} %compare.3, pred[]{:T(512)S(6)} %gt.12), kind=kOutput, calls=%fused_computation.3.clone.1 | convolution fusion | flops 679919616 | bytes 2951168 | tf_op jit(solution)/shard_map/while/body/eval_jaxpr/sik,slk->sil/dot_general | solution.py:30
  136.7 2.0 fusion.14
  138.8 2.0 convolution_add_fusion.2
  140.8 2.9 %fusion.23 = f32[384,384]{1,0:T(8,128)} fusion(f32[384,384]{1,0:T(8,128)S(1)} %convolution_add_fusion.2, f32[2,1,384,384]{3,2,1,0:T(8,128)S(1)} %copy-done), kind=kOutput, calls=%fused_computation.30 | convolution fusion | flops 679477248 | bytes 1769472 | tf_op jit(solution)/shard_map/sij,sjk->sik/dot_general | solution.py:28
  143.7 1.4 stack.19
  145.1 3.1 %convolution_add_fusion.1 = f32[384,384]{1,0:T(8,128)S(1)} fusion(f32[384,384]{1,0:T(8,128)} %fusion.23, f32[2,1,384,384]{3,2,1,0:T(8,128)S(1)} %copy-done.1, f32[2,1,384,384]{3,2,1,0:T(8,128)S(1)} %copy-done), kind=kOutput, calls=%fused_computation.16 | convolution fusion | flops 679624704 | bytes 2359296 | tf_op jit(solution)/shard_map/sik,slk->sil/dot_general | solution.py:30
  148.2 0.6 stack.18
  148.8 0.5 copy-done.2
  149.3 1.1 maximum_bitcast_fusion
  150.4 34.9 %gather_fusion = f32[4096]{0:T(1024)S(1)} fusion(f32[2,147456]{1,0:T(2,128)S(1)} %maximum_bitcast_fusion, s32[4096]{0:T(1024)S(1)} %bitcast.81), kind=kCustom, calls=%fused_computation | custom fusion | bytes 65536 | tf_op jit(solution)/shard_map/jit(take_along_axis)/gather | solution.py:66
  185.4 0.1 select_reduce_fusion
  185.6 6.4 %psum.14 = f32[4]{0:T(128)S(1)} all-reduce(f32[4]{0:T(128)S(1)} %broadcast_multiply_fusion), channel_id=1, replica_groups=mesh['fits'=2,'tm'=4,'space'=4] {'space'}, use_global_device_ids=true, to_apply=%region_3.4 | all-reduce | flops 4 | bytes 32 | tf_op jit(solution)/shard_map/psum | solution.py:69
  192.0 10.4 %psum.15 = f32[4]{0:T(128)} all-reduce(f32[4]{0:T(128)S(1)} %psum.14), channel_id=1, replica_groups=mesh['fits'=2,'tm'=4,'space'=4] {'tm'}, use_global_device_ids=true, to_apply=%region_4.5 | all-reduce | flops 4 | bytes 32 | tf_op jit(solution)/shard_map/psum | solution.py:69
  202.4 1.1 pad_maximum_fusion
  (22 shorter events, 0.1 us)
Async XLA Ops:
  7.2 2.7 %copy-start = (f32[2,1,384,384]{3,2,1,0:T(8,128)S(1)}, f32[2,1,384,384]{3,2,1,0:T(8,128)}, u32[]{:S(2)}) copy-start(f32[2,1,384,384]{3,2,1,0:T(8,128)} %param.8) | copy-start | bytes 3538948
  7.2 58.7 %all-gather.7.cloned.1.call-start = ((), (), s32[]{:S(2)}) async-start(), calls=%async_computation.1 | async-start | bytes 2949120 | tf_op jit(solution)/shard_map/all_gather | solution.py:11
  13.0 2.2 %copy-start.5 = (s32[2,1,2048]{2,1,0:T(1,128)S(1)}, s32[2,1,2048]{2,1,0:T(1,128)}, u32[]{:S(2)}) copy-start(s32[2,1,2048]{2,1,0:T(1,128)} %param.12) | copy-start | bytes 49156
  13.0 2.8 %copy-start.6 = (s32[2,1,2048]{2,1,0:T(1,128)S(1)}, s32[2,1,2048]{2,1,0:T(1,128)}, u32[]{:S(2)}) copy-start(s32[2,1,2048]{2,1,0:T(1,128)} %param.10) | copy-start | bytes 49156
  13.0 2.8 %copy-start.7 = (s32[2,1,2048]{2,1,0:T(1,128)S(1)}, s32[2,1,2048]{2,1,0:T(1,128)}, u32[]{:S(2)}) copy-start(s32[2,1,2048]{2,1,0:T(1,128)} %param.11) | copy-start | bytes 49156
  13.0 103.7 %all-gather.5.cloned.1.call-start = ((), (), s32[]{:S(2)}) async-start(), calls=%async_computation | async-start | bytes 2949120 | tf_op jit(solution)/shard_map/all_gather | solution.py:11
  136.7 2.1 copy-start.1
  148.2 1.1 copy-start.2
  150.4 35.0 %copy-start.4 = (s32[2,1,2048]{2,1,0:T(1,128)S(1)}, s32[2,1,2048]{2,1,0:T(1,128)}, u32[]{:S(2)}) copy-start(s32[2,1,2048]{2,1,0:T(1,128)} %get-tuple-element.179) | copy-start | bytes 49156
  150.4 35.0 %copy-start.8 = (f32[2,1,2048]{2,1,0:T(1,128)S(1)}, f32[2,1,2048]{2,1,0:T(1,128)}, u32[]{:S(2)}) copy-start(f32[2,1,2048]{2,1,0:T(1,128)} %param.13) | copy-start | bytes 49156
  150.4 35.0 %copy-start.3 = (s32[2,1,2048]{2,0,1:T(2,128)S(1)}, s32[2,1,2048]{2,0,1:T(2,128)}, u32[]{:S(2)}) copy-start(s32[2,1,2048]{2,0,1:T(2,128)} %copy.23) | copy-start | bytes 49156
Sparse Core Ops, SparseCore 0:
  13.1 52.6 all-gather.6
  68.0 48.7 all-gather.4
